TPU v7x, 32 devices: a whole 2x2x4 slice. The times are simulated.
32 devices in a mesh: sensor: 4 (over y, core), space: 8 (over z, x).
Axes of the slice: x: 2, y: 2, z: 4, core: 2. Of those that a mesh axis runs over, the one named last changes fastest.
Arguments:
- jacobian: float32 [512, 16384], P('space', 'sensor'), as said below
- residual: float32 [16384], P('sensor'), may hold values from -6 to 6
- damping: float32 [1], replicated, may hold values from 0.3 to 3
Outputs:
- update: float32 [512], replicated
Inputs may be any that keep to these rules, and one draw needn't show every extreme that they name: `jacobian`: every column block of the Jacobian has full rank over any 512 observations, which number at least the parameters; the entries are real-valued with row and column scales that vary.
All inputs are finite; a program needn't handle non-finite values.
Results may differ from a plain program's by a relative error of at most 0.00011.
Values sent between devices are 32-bit elements; how exact they have to be, the bound alone decides.
No kernel may reach another device: no remote copies, remote signals or barrier semaphores. Data moves between devices by JAX's collectives and lax.ppermute only.
A program may use at most 64 MiB of HBM per device.

v0:
```python
import jax
import jax.numpy as jnp
from jax import lax
from jax.sharding import PartitionSpec as P


def per_device(jacobian, residual, damping):
    high = lax.Precision.HIGHEST
    columns = jacobian.shape[0]
    groups = lax.axis_size("space")
    params_all = columns * groups
    part_grad = jnp.dot(jacobian, residual, precision=high)
    grad_local = lax.dynamic_update_slice(
        jnp.zeros((params_all,), jnp.float32), part_grad, (lax.axis_index("space") * columns,)
    )
    panel_t = lax.all_to_all(jacobian, "space", split_axis=1, concat_axis=0, tiled=True)
    gram_local = lax.dot_general(panel_t, panel_t, (((1,), (1,)), ((), ())), precision=high)
    gram_group, grad_group = lax.psum((gram_local, grad_local), "space")
    gram_all, grad_all = lax.psum((gram_group, grad_group), "sensor")
    damped = gram_all + damping[0] * jnp.diag(jnp.diag(gram_all))
    factor = jnp.linalg.cholesky(damped)
    return -jax.scipy.linalg.cho_solve((factor, True), grad_all)


def solution(mesh):
    placed = (P("space", "sensor"), P("sensor"), P())
    return jax.shard_map(per_device, mesh=mesh, in_specs=placed, out_specs=P(), check_vma=False)
```

profile of v0, /device:TPU:0, one launch (start us, length us, event | category | flops | bytes accessed | tf_op | source)
XLA Modules:
  0.0 311.7 jit_solution(12249171158985935714)
XLA Ops:
  6.5 1.3 copy.52
  7.9 32.8 %all_to_all.19 = f32[64,8,512]{2,0,1:T(8,128)S(1)} all-to-all(f32[64,8,512]{2,0,1:T(8,128)S(1)} %bitcast.158), channel_id=1, replica_groups=mesh['sensor'=4,'space'=8] {'space'}, dimensions={1} | all-to-all | bytes 2097152 | tf_op jit(solution)/shard_map/all_to_all | solution.py:16
  40.7 2.9 fusion.57
  43.7 77.3 %all-reduce.4.cloned.1.call-done = f32[512,512]{0,1:T(8,128)} async-done(((f32[512,512]{0,1:T(8,128)}), f32[512,512]{0,1:T(8,128)}) %all-reduce.4.cloned.1.call-update) | async-done | bytes 1048592 | tf_op jit(solution)/shard_map/psum | solution.py:18
  121.7 0.9 convolution_bitcast_fusion
  122.8 20.0 %psum.30 = f32[512]{0:T(512)S(1)} all-reduce(f32[512]{0:T(512)S(1)} %dynamic_update_slice.3), channel_id=1, replica_groups=mesh['sensor'=4,'space'=8] {'space'}, use_global_device_ids=true, to_apply=%region_10.11 | all-reduce | flops 512 | bytes 4096 | tf_op jit(solution)/shard_map/psum | solution.py:18
  142.8 5.6 %psum.31 = f32[512]{0:T(512)S(1)} all-reduce(f32[512]{0:T(512)S(1)} %psum.30), channel_id=1, replica_groups=mesh['sensor'=4,'space'=8] {'sensor'}, use_global_device_ids=true, to_apply=%region_11.12 | all-reduce | flops 512 | bytes 4096 | tf_op jit(solution)/shard_map/psum | solution.py:19
  148.5 10.8 %all-reduce.6.cloned.1.call-done = f32[512,512]{0,1:T(8,128)} async-done(((f32[512,512]{0,1:T(8,128)}), f32[512,512]{0,1:T(8,128)}) %all-reduce.6.cloned.1.call-update) | async-done | bytes 1048592 | tf_op jit(solution)/shard_map/psum | solution.py:19
  159.3 8.7 %gather_fusion = f32[512]{0:T(512)S(1)} fusion(f32[512,512]{0,1:T(8,128)} %all-reduce.6.cloned.1.call-done, s32[512]{0:T(512)S(1)} %bitcast.155), kind=kCustom, calls=%fused_computation | custom fusion | bytes 8192 | tf_op jit(solution)/shard_map/jit(_diag)/jit(diagonal)/cond/branch_0_fun/gather | solution.py:20
  168.7 11.7 %cholesky.103 = f32[128,128]{1,0:T(8,128)S(1)} custom-call(f32[128,128]{1,0:T(8,128)S(1)} %cholesky.263), custom_call_target="Cholesky" | custom-call | tf_op jit(solution)/shard_map/jit(cholesky)/cholesky | solution.py:21
  180.6 9.8 %custom-call.34 = f32[1,128,128]{1,2,0:T(8,128)S(1)} custom-call(f32[1,128,128]{2,1,0:T(8,128)S(1)} %get-tuple-element.44), custom_call_target="InvertDiagBlocksLowerTriangular" | custom-call | tf_op jit(solution)/shard_map/jit(cholesky)/cholesky | solution.py:21
  191.2 11.7 %cholesky.215 = f32[128,128]{1,0:T(8,128)S(1)} custom-call(f32[128,128]{1,0:T(8,128)S(1)} %cholesky.267), custom_call_target="Cholesky" | custom-call | tf_op jit(solution)/shard_map/jit(cholesky)/cholesky | solution.py:21
  203.2 10.0 %custom-call.35 = f32[1,128,128]{1,2,0:T(8,128)S(1)} custom-call(f32[1,128,128]{2,1,0:T(8,128)S(1)} %get-tuple-element.42), custom_call_target="InvertDiagBlocksLowerTriangular" | custom-call | tf_op jit(solution)/shard_map/jit(cholesky)/cholesky | solution.py:21
  213.5 0.6 convolution_subtract_fusion.1
  214.1 11.7 %cholesky.236 = f32[128,128]{1,0:T(8,128)S(1)} custom-call(f32[128,128]{1,0:T(8,128)S(1)} %cholesky.272), custom_call_target="Cholesky" | custom-call | tf_op jit(solution)/shard_map/jit(cholesky)/cholesky | solution.py:21
  226.0 9.8 %custom-call.36 = f32[1,128,128]{1,2,0:T(8,128)S(1)} custom-call(f32[1,128,128]{2,1,0:T(8,128)S(1)} %get-tuple-element.40), custom_call_target="InvertDiagBlocksLowerTriangular" | custom-call | tf_op jit(solution)/shard_map/jit(cholesky)/cholesky | solution.py:21
  236.1 0.5 convolution_subtract_fusion.2
  236.6 11.9 %cholesky.253 = f32[128,128]{1,0:T(8,128)S(1)} custom-call(f32[128,128]{1,0:T(8,128)S(1)} %convolution_subtract_fusion.2), custom_call_target="Cholesky" | custom-call | tf_op jit(solution)/shard_map/jit(cholesky)/cholesky | solution.py:21
  248.7 0.7 compare_reduce_fusion.1
  249.4 0.6 compare_reduce_fusion
  250.1 0.7 compare_reduce_fusion.2
  253.4 8.6 %while.1 = (s32[]{:T(128)}, f32[512,512]{0,1:T(8,128)S(1)}, s32[4,2]{0,1:T(2,128)S(1)}, f32[4,128,128]{2,1,0:T(8,128)S(1)}, s32[]{:T(128)}) while((s32[]{:T(128)}, f32[512,512]{0,1:T(8,128)S(1)}, s32[4,2]{0,1:T(2,128)S(1)}, f32[4,128,128]{2,1,0:T(8,128)S(1)}, s32[]{:T(128)}) %tuple.27), condition=%wide.while_cond, body=%wide.while_body.sunk | while | flops 2 | bytes 393329 | solution.py:22
  253.5 0.6 fusion.72
  254.1 1.3 dynamic-slice.7
  255.7 0.6 fusion.72
  256.3 1.3 dynamic-slice.7
  257.8 0.6 fusion.72
  258.4 1.3 dynamic-slice.7
  260.0 0.6 fusion.72
  260.6 1.3 dynamic-slice.7
  262.0 39.3 %custom-call.37 = f32[4,128,128]{1,2,0:T(8,128)S(1)} custom-call(f32[4,128,128]{2,1,0:T(8,128)S(1)} %get-tuple-element.12), custom_call_target="InvertDiagBlocksLowerTriangular" | custom-call | tf_op jit(solution)/shard_map/jit(_cho_solve)/triangular_solve | solution.py:22
  304.3 0.6 maximum_negate_fusion
  (67 shorter events, 6.8 us)
Async XLA Ops:
  6.5 115.1 %copy-start = (f32[4096]{0:T(1024)S(1)}, f32[4096]{0:T(1024)}, u32[]{:S(2)}) copy-start(f32[4096]{0:T(1024)} %param.4) | copy-start | bytes 49156
  6.5 114.4 %all-reduce.4.cloned.1.call-start = ((), (), s32[]{:S(2)}) async-start(), calls=%async_computation.1 | async-start | bytes 2097152 | tf_op jit(solution)/shard_map/psum | solution.py:18
  43.6 78.1 %copy-start.2 = (f32[64,4096]{1,0:T(8,128)S(1)}, f32[64,4096]{1,0:T(8,128)}, u32[]{:S(2)}) copy-start(f32[64,4096]{1,0:T(8,128)} %param.3) | copy-start | bytes 3145732
  43.6 115.6 %all-reduce.6.cloned.1.call-start = ((), (), s32[]{:S(2)}) async-start(), calls=%async_computation.2 | async-start | bytes 2097152 | tf_op jit(solution)/shard_map/psum | solution.py:19
  159.3 8.7 %copy-start.1 = (f32[512,512]{0,1:T(8,128)S(1)}, f32[512,512]{0,1:T(8,128)}, u32[]{:S(2)}) copy-start(f32[512,512]{0,1:T(8,128)} %all-reduce.6.cloned.1.call-done) | copy-start | bytes 3145732
Sparse Core Ops, SparseCore 0:
  43.8 77.1 all-reduce.3
  123.3 35.8 all-reduce.5
where the time goes:
time: 312 us
  other arithmetic  119 us (38%)
  waiting for transfers between devices  88.1 us (28%)
  blocking collectives  58.5 us (19%)
  local copies, waits for them, and re-layouts  19.7 us (6%)
  between operations  16.9 us (5%)
  matrix products  9.06 us (3%)
    another operation x14, other arithmetic, per_device(): factor = jnp.linalg.cholesky(damped)  78.9 us
    psum x1, waiting for transfers between devices, per_device(): gram_group, grad_group = lax.psum((gram_local, grad_local), 'space')  77.3 us
    another operation x3, other arithmetic, per_device(): return -jax.scipy.linalg.cho_solve((factor, True), grad_all)  39.4 us
    all_to_all x1, blocking collectives, per_device(): lax.all_to_all(jacobian, 'space', split_axis=1, concat_axis=0, tiled=True)  32.8 us
    psum x1, blocking collectives, per_device(): gram_group, grad_group = lax.psum((gram_local, grad_local), 'space')  20 us
    psum x1, waiting for transfers between devices, per_device(): gram_all, grad_all = lax.psum((gram_group, grad_group), 'sensor')  10.8 us
    gather x1, local copies, waits for them, and re-layouts, per_device(): damped = gram_all + damping[0] * jnp.diag(jnp.diag(gram_all))  8.67 us
    another operation x20, local copies, waits for them, and re-layouts  8.46 us
  transfers between devices with their start and end apart: 2, of which 2 were waited for; matrix products, arithmetic and copies ran while one was open for 0% of the time, Pallas kernels for 0%

commit v1 on v0

--- a/solution.py
+++ b/solution.py
@@ -2,6 +2,18 @@
 import jax.numpy as jnp
 from jax import lax
 from jax.sharding import PartitionSpec as P
+
+
+def split_up(x, dim, size):
+    shape = x.shape
+    parts = x.reshape(*shape[:dim], size, shape[dim] // size, *shape[dim + 1 :])
+    return jnp.moveaxis(parts, dim, 0)
+
+
+def in_order(blocks, dim):
+    blocks = jnp.moveaxis(blocks, 0, dim)
+    lengths = blocks.shape
+    return blocks.reshape(*lengths[:dim], lengths[dim] * lengths[dim + 1], *lengths[dim + 2 :])
 
 
 def per_device(jacobian, residual, damping):
@@ -13,7 +25,14 @@
     grad_local = lax.dynamic_update_slice(
         jnp.zeros((params_all,), jnp.float32), part_grad, (lax.axis_index("space") * columns,)
     )
-    panel_t = lax.all_to_all(jacobian, "space", split_axis=1, concat_axis=0, tiled=True)
+    size, index = (lax.axis_size("space"), lax.axis_index("space"))
+    tiles = split_up(jacobian, 1, size)
+    gathered = [tiles[index]]
+    for step in range(1, size):
+        sent = tiles[(index + step) % size]
+        gathered.append(lax.ppermute(sent, "space", [(i, (i + step) % size) for i in range(size)]))
+    tiles = jnp.stack(gathered)[(index - jnp.arange(size)) % size]
+    panel_t = in_order(tiles, 0)
     gram_local = lax.dot_general(panel_t, panel_t, (((1,), (1,)), ((), ())), precision=high)
     gram_group, grad_group = lax.psum((gram_local, grad_local), "space")
     gram_all, grad_all = lax.psum((gram_group, grad_group), "sensor")

time: 312 us -> 312 us (level)
  blocking collectives: 58.5 us -> 25.7 us
  waiting for transfers between devices: 88.1 us -> 103 us
  starting transfers between devices: 0.04 us -> 14.3 us
    all_to_all x1 -> x0, blocking collectives: 32.8 us -> none  [per_device(): lax.all_to_all(jacobian, 'space', split_axis=1, concat_axis=0, tiled=True)]
    ppermute x0 -> x7, starting transfers between devices: none -> 14.3 us  [per_device(): lax.ppermute(sent, 'space', [(i, (i + step) % size) for i in range(size)])]
    psum x1, waiting for transfers between devices: 77.3 us -> 85.7 us  [per_device(): gram_group, grad_group = lax.psum((gram_local, grad_local), 'space')]
    ppermute x0 -> x7, waiting for transfers between devices: none -> 6.86 us  [per_device(): lax.ppermute(sent, 'space', [(i, (i + step) % size) for i in range(size)])]
    another operation x20 -> x22, local copies, waits for them, and re-layouts: 8.46 us -> 9.53 us
  transfers between devices with their start and end apart: 2 -> 9, of which waited for: 2 -> 4; matrix products, arithmetic and copies ran while one was open for 0% -> 0% of each run, Pallas kernels for 0% -> 0%
where the time goes in v1:
time: 312 us; the launch traced here: 311 us
  other arithmetic  119 us (38%)
  waiting for transfers between devices  103 us (33%)
  blocking collectives  25.7 us (8%)
  local copies, waits for them, and re-layouts  22 us (7%)
  between operations  17 us (5%)
  starting transfers between devices  14.3 us (5%)
  matrix products  9.05 us (3%)
    psum x1, waiting for transfers between devices, per_device(): gram_group, grad_group = lax.psum((gram_local, grad_local), 'space')  85.7 us
    another operation x14, other arithmetic, per_device(): factor = jnp.linalg.cholesky(damped)  78.9 us
    another operation x3, other arithmetic, per_device(): return -jax.scipy.linalg.cho_solve((factor, True), grad_all)  39.4 us
    psum x1, blocking collectives, per_device(): gram_group, grad_group = lax.psum((gram_local, grad_local), 'space')  20 us
    ppermute x7, starting transfers between devices, per_device(): lax.ppermute(sent, 'space', [(i, (i + step) % size) for i in range(size)])  14.3 us
    psum x1, waiting for transfers between devices, per_device(): gram_all, grad_all = lax.psum((gram_group, grad_group), 'sensor')  10.8 us
    another operation x21, local copies, waits for them, and re-layouts  9.52 us
    gather x1, local copies, waits for them, and re-layouts, per_device(): damped = gram_all + damping[0] * jnp.diag(jnp.diag(gram_all))  8.67 us
  transfers between devices with their start and end apart: 9, of which 4 were waited for; matrix products, arithmetic and copies ran while one was open for 0% of the time, Pallas kernels for 0%

profile of v1, /device:TPU:0, one launch (start us, length us, event | category | flops | bytes accessed | tf_op | source)
XLA Modules:
  0.0 311.1 jit_solution(12578675553524134155)
XLA Ops:
  6.5 1.8 copy.36
  8.4 1.1 constant_dynamic-slice_fusion.1
  9.5 3.0 collective-permute-start
  12.5 1.6 collective-permute-start.1
  14.2 2.6 collective-permute-start.2
  16.8 1.3 collective-permute-start.3
  18.1 2.7 collective-permute-start.4
  20.9 1.4 collective-permute-start.5
  22.3 1.7 collective-permute-start.6
  24.0 6.4 %collective-permute-done.2 = f32[64,512]{1,0:T(8,128)S(1)} collective-permute-done((f32[64,512]{1,0:T(8,128)S(1)}, f32[64,512]{1,0:T(8,128)S(1)}, u32[]{:S(2)}, u32[]{:S(2)}) %collective-permute-start.2) | collective-permute-done | bytes 131104 | tf_op jit(solution)/shard_map/ppermute | solution.py:33
  31.6 2.9 fusion.59
  34.5 85.7 %all-reduce.4.cloned.1.call-done = f32[512,512]{0,1:T(8,128)} async-done(((f32[512,512]{0,1:T(8,128)}), f32[512,512]{0,1:T(8,128)}) %all-reduce.4.cloned.1.call-update) | async-done | bytes 1048592 | tf_op jit(solution)/shard_map/psum | solution.py:37
  121.0 0.9 convolution_bitcast_fusion
  122.1 20.0 %psum.30 = f32[512]{0:T(512)S(1)} all-reduce(f32[512]{0:T(512)S(1)} %dynamic_update_slice.3), channel_id=1, replica_groups=mesh['sensor'=4,'space'=8] {'space'}, use_global_device_ids=true, to_apply=%region_10.11 | all-reduce | flops 512 | bytes 4096 | tf_op jit(solution)/shard_map/psum | solution.py:37
  142.1 5.6 %psum.31 = f32[512]{0:T(512)S(1)} all-reduce(f32[512]{0:T(512)S(1)} %psum.30), channel_id=1, replica_groups=mesh['sensor'=4,'space'=8] {'sensor'}, use_global_device_ids=true, to_apply=%region_11.12 | all-reduce | flops 512 | bytes 4096 | tf_op jit(solution)/shard_map/psum | solution.py:38
  147.8 10.8 %all-reduce.6.cloned.1.call-done = f32[512,512]{0,1:T(8,128)} async-done(((f32[512,512]{0,1:T(8,128)}), f32[512,512]{0,1:T(8,128)}) %all-reduce.6.cloned.1.call-update) | async-done | bytes 1048592 | tf_op jit(solution)/shard_map/psum | solution.py:38
  158.6 8.7 %gather_fusion.1 = f32[512]{0:T(512)S(1)} fusion(f32[512,512]{0,1:T(8,128)} %all-reduce.6.cloned.1.call-done, s32[512]{0:T(512)S(1)} %bitcast.190), kind=kCustom, calls=%fused_computation.1 | custom fusion | bytes 8192 | tf_op jit(solution)/shard_map/jit(_diag)/jit(diagonal)/cond/branch_0_fun/gather | solution.py:39
  168.0 11.7 %cholesky.103 = f32[128,128]{1,0:T(8,128)S(1)} custom-call(f32[128,128]{1,0:T(8,128)S(1)} %cholesky.263), custom_call_target="Cholesky" | custom-call | tf_op jit(solution)/shard_map/jit(cholesky)/cholesky | solution.py:40
  179.9 9.8 %custom-call.34 = f32[1,128,128]{1,2,0:T(8,128)S(1)} custom-call(f32[1,128,128]{2,1,0:T(8,128)S(1)} %get-tuple-element.44), custom_call_target="InvertDiagBlocksLowerTriangular" | custom-call | tf_op jit(solution)/shard_map/jit(cholesky)/cholesky | solution.py:40
  190.5 11.7 %cholesky.215 = f32[128,128]{1,0:T(8,128)S(1)} custom-call(f32[128,128]{1,0:T(8,128)S(1)} %cholesky.267), custom_call_target="Cholesky" | custom-call | tf_op jit(solution)/shard_map/jit(cholesky)/cholesky | solution.py:40
  202.5 10.0 %custom-call.35 = f32[1,128,128]{1,2,0:T(8,128)S(1)} custom-call(f32[1,128,128]{2,1,0:T(8,128)S(1)} %get-tuple-element.42), custom_call_target="InvertDiagBlocksLowerTriangular" | custom-call | tf_op jit(solution)/shard_map/jit(cholesky)/cholesky | solution.py:40
  213.5 11.7 %cholesky.236 = f32[128,128]{1,0:T(8,128)S(1)} custom-call(f32[128,128]{1,0:T(8,128)S(1)} %cholesky.272), custom_call_target="Cholesky" | custom-call | tf_op jit(solution)/shard_map/jit(cholesky)/cholesky | solution.py:40
  225.3 9.8 %custom-call.36 = f32[1,128,128]{1,2,0:T(8,128)S(1)} custom-call(f32[1,128,128]{2,1,0:T(8,128)S(1)} %get-tuple-element.40), custom_call_target="InvertDiagBlocksLowerTriangular" | custom-call | tf_op jit(solution)/shard_map/jit(cholesky)/cholesky | solution.py:40
  235.9 11.9 %cholesky.253 = f32[128,128]{1,0:T(8,128)S(1)} custom-call(f32[128,128]{1,0:T(8,128)S(1)} %convolution_subtract_fusion.2), custom_call_target="Cholesky" | custom-call | tf_op jit(solution)/shard_map/jit(cholesky)/cholesky | solution.py:40
  248.0 0.7 compare_reduce_fusion.1
  249.4 0.7 compare_reduce_fusion.2
  252.7 8.6 %while.1 = (s32[]{:T(128)}, f32[512,512]{0,1:T(8,128)S(1)}, s32[4,2]{0,1:T(2,128)S(1)}, f32[4,128,128]{2,1,0:T(8,128)S(1)}, s32[]{:T(128)}) while((s32[]{:T(128)}, f32[512,512]{0,1:T(8,128)S(1)}, s32[4,2]{0,1:T(2,128)S(1)}, f32[4,128,128]{2,1,0:T(8,128)S(1)}, s32[]{:T(128)}) %tuple.32), condition=%wide.while_cond, body=%wide.while_body.sunk | while | flops 2 | bytes 393329 | solution.py:41
  253.4 1.3 dynamic-slice.47
  255.6 1.3 dynamic-slice.47
  257.7 1.3 dynamic-slice.47
  259.9 1.3 dynamic-slice.47
  261.3 39.3 %custom-call.37 = f32[4,128,128]{1,2,0:T(8,128)S(1)} custom-call(f32[4,128,128]{2,1,0:T(8,128)S(1)} %get-tuple-element.12), custom_call_target="InvertDiagBlocksLowerTriangular" | custom-call | tf_op jit(solution)/shard_map/jit(_cho_solve)/triangular_solve | solution.py:41
  (99 shorter events, 12.8 us)
Async XLA Ops:
  6.5 114.4 %copy-start = (f32[4096]{0:T(1024)S(1)}, f32[4096]{0:T(1024)}, u32[]{:S(2)}) copy-start(f32[4096]{0:T(1024)} %param.4) | copy-start | bytes 49156
  6.5 113.8 %all-reduce.4.cloned.1.call-start = ((), (), s32[]{:S(2)}) async-start(), calls=%async_computation | async-start | bytes 2097152 | tf_op jit(solution)/shard_map/psum | solution.py:37
  9.5 11.4 %collective-permute-start = (f32[64,512]{1,0:T(8,128)S(1)}, f32[64,512]{1,0:T(8,128)S(1)}, u32[]{:S(2)}, u32[]{:S(2)}) collective-permute-start(f32[64,512]{1,0:T(8,128)S(1)} %bitcast.200), channel_id=1, source_target_pairs={{0,1},{1,2},{2,3},{3,4},{4,5},{5,6},{6,7},{7,0},{8,9},{9,10},{10,1... | collective-permute-start | bytes 393224 | tf_op jit(solution)/shard_map/ppermute | solution.py:33
  12.5 9.8 %collective-permute-start.1 = (f32[64,512]{1,0:T(8,128)S(1)}, f32[64,512]{1,0:T(8,128)S(1)}, u32[]{:S(2)}, u32[]{:S(2)}) collective-permute-start(f32[64,512]{1,0:T(8,128)S(1)} %bitcast.199), channel_id=1, source_target_pairs={{0,2},{1,3},{2,4},{3,5},{4,6},{5,7},{6,0},{7,1},{8,10},{9,11},{10,... | collective-permute-start | bytes 393224 | tf_op jit(solution)/shard_map/ppermute | solution.py:33
  14.2 16.2 %collective-permute-start.2 = (f32[64,512]{1,0:T(8,128)S(1)}, f32[64,512]{1,0:T(8,128)S(1)}, u32[]{:S(2)}, u32[]{:S(2)}) collective-permute-start(f32[64,512]{1,0:T(8,128)S(1)} %bitcast.197), channel_id=1, source_target_pairs={{0,3},{1,4},{2,5},{3,6},{4,7},{5,0},{6,1},{7,2},{8,11},{9,12},{10,... | collective-permute-start | bytes 393224 | tf_op jit(solution)/shard_map/ppermute | solution.py:33
  16.8 14.0 %collective-permute-start.3 = (f32[64,512]{1,0:T(8,128)S(1)}, f32[64,512]{1,0:T(8,128)S(1)}, u32[]{:S(2)}, u32[]{:S(2)}) collective-permute-start(f32[64,512]{1,0:T(8,128)S(1)} %bitcast.196), channel_id=1, source_target_pairs={{0,4},{1,5},{2,6},{3,7},{4,0},{5,1},{6,2},{7,3},{8,12},{9,13},{10,... | collective-permute-start | bytes 393224 | tf_op jit(solution)/shard_map/ppermute | solution.py:33
  18.1 12.7 %collective-permute-start.4 = (f32[64,512]{1,0:T(8,128)S(1)}, f32[64,512]{1,0:T(8,128)S(1)}, u32[]{:S(2)}, u32[]{:S(2)}) collective-permute-start(f32[64,512]{1,0:T(8,128)S(1)} %bitcast.195), channel_id=1, source_target_pairs={{0,5},{1,6},{2,7},{3,0},{4,1},{5,2},{6,3},{7,4},{8,13},{9,14},{10,... | collective-permute-start | bytes 393224 | tf_op jit(solution)/shard_map/ppermute | solution.py:33
  20.9 10.0 %collective-permute-start.5 = (f32[64,512]{1,0:T(8,128)S(1)}, f32[64,512]{1,0:T(8,128)S(1)}, u32[]{:S(2)}, u32[]{:S(2)}) collective-permute-start(f32[64,512]{1,0:T(8,128)S(1)} %bitcast.198), channel_id=1, source_target_pairs={{0,6},{1,7},{2,0},{3,1},{4,2},{5,3},{6,4},{7,5},{8,14},{9,15},{10,... | collective-permute-start | bytes 393224 | tf_op jit(solution)/shard_map/ppermute | solution.py:33
  22.3 8.6 %collective-permute-start.6 = (f32[64,512]{1,0:T(8,128)S(1)}, f32[64,512]{1,0:T(8,128)S(1)}, u32[]{:S(2)}, u32[]{:S(2)}) collective-permute-start(f32[64,512]{1,0:T(8,128)S(1)} %bitcast.194), channel_id=1, source_target_pairs={{0,7},{1,0},{2,1},{3,2},{4,3},{5,4},{6,5},{7,6},{8,15},{9,8},{10,9... | collective-permute-start | bytes 393224 | tf_op jit(solution)/shard_map/ppermute | solution.py:33
  34.5 86.5 %copy-start.2 = (f32[64,4096]{1,0:T(8,128)S(1)}, f32[64,4096]{1,0:T(8,128)}, u32[]{:S(2)}) copy-start(f32[64,4096]{1,0:T(8,128)} %param.3) | copy-start | bytes 3145732
  34.5 124.1 %all-reduce.6.cloned.1.call-start = ((), (), s32[]{:S(2)}) async-start(), calls=%async_computation.1 | async-start | bytes 2097152 | tf_op jit(solution)/shard_map/psum | solution.py:38
  158.6 8.7 %copy-start.1 = (f32[512,512]{0,1:T(8,128)S(1)}, f32[512,512]{0,1:T(8,128)}, u32[]{:S(2)}) copy-start(f32[512,512]{0,1:T(8,128)} %all-reduce.6.cloned.1.call-done) | copy-start | bytes 3145732
Sparse Core Ops, SparseCore 0:
  34.6 85.6 all-reduce.3
  122.7 35.8 all-reduce.5
